TPU v7x, 32 devices: a whole 2x2x4 slice. The times are simulated.
32 devices in a mesh: grid: 8 (over z, y), vec: 4 (over x, core).
Axes of the slice: x: 2, y: 2, z: 4, core: 2. Of those that a mesh axis runs over, the one named last changes fastest.
Arguments:
- trial_block: float32 [16, 48, 32, 128], P('vec', 'grid'), may hold values from -60 to 60, as said below
- response_weight: float32 [48, 32, 128], P('grid'), may hold values from 2 to 5
Outputs:
- rotated: float32 [16, 48, 32, 128], P('vec', 'grid')
- potentials: float32 [16, 48, 32, 128], P('vec', 'grid')
- ritz_matrix: float32 [16, 16], replicated
Inputs may be any that keep to these rules, and one draw needn't show every extreme that they name: `trial_block`: trial vectors whose Gram matrix is positive definite.
All inputs are finite; a program needn't handle non-finite values.
Results may differ from a plain program's by a relative error of at most 0.0002.
Values sent between devices are 32-bit elements; how exact they have to be, the bound alone decides.
A program may use at most 64 MiB of HBM per device.

v0:
```python
import jax
import jax.numpy as jnp
from jax import lax
from jax.sharding import PartitionSpec as P

ITERS = 3


COEFFS = (
    -5369.0 / 1800.0,
    12.0 / 7.0,
    -15.0 / 56.0,
    10.0 / 189.0,
    -1.0 / 112.0,
    2.0 / 1925.0,
    -1.0 / 16632.0,
)


def shifted(value, axis, steps):
    count = lax.axis_size(axis)
    pairs = [(source, (source + steps) % count) for source in range(count)]
    return lax.ppermute(value, axis, pairs)


def with_halo(cells, sides, width):
    for axis, dim in sides:
        count = lax.axis_size(axis)
        head = lax.slice_in_dim(cells, 0, width, axis=dim)
        tail = lax.slice_in_dim(cells, cells.shape[dim] - width, cells.shape[dim], axis=dim)
        cells = jnp.concatenate(
            [
                lax.ppermute(tail, axis, [(i, (i + 1) % count) for i in range(count)]),
                cells,
                lax.ppermute(head, axis, [((i + 1) % count, i) for i in range(count)]),
            ],
            axis=dim,
        )
    return cells


def along_axis(total, padded, axis, length):
    for offset in range(1, 7):
        upper = lax.slice_in_dim(padded, 6 + offset, 6 + offset + length, axis=axis)
        lower = lax.slice_in_dim(padded, 6 - offset, 6 - offset + length, axis=axis)
        total = total + COEFFS[offset] * (upper + lower)
    return total


def operate(field):
    stride = max(lax.axis_size("grid") // 16, 2)
    row_count = field.shape[1]
    col_count = field.shape[2]
    total = 3.0 * COEFFS[0] * field
    below = shifted(field, "grid", stride)
    above = shifted(field, "grid", -stride)
    along_x = jnp.concatenate([below, field, above], axis=1)
    total = along_axis(total, along_x, 1, row_count)
    side_halo = with_halo(field, (("grid", 2),), 6)
    total = along_axis(total, side_halo, 2, col_count)
    along_z = jnp.pad(field, ((0, 0), (0, 0), (0, 0), (6, 6)))
    total = along_axis(total, along_z, 3, field.shape[3])
    return -total


def inner(left, right):
    return jnp.sum(left * right, axis=(1, 2, 3))


def expand(values):
    return values[:, None, None, None]


def two_products(residual, image):
    return lax.psum((inner(residual, residual), inner(residual, image)), "grid")


def finish(gram, cross, cells):
    high = lax.Precision.HIGHEST
    gram = gram / cells
    cross = cross / cells
    lower = jnp.linalg.cholesky(gram)
    inverse = lax.linalg.triangular_solve(
        lower, jnp.eye(gram.shape[0], dtype=jnp.float32), left_side=True, lower=True
    )
    middle = jnp.dot(inverse, 0.5 * (cross + cross.T), precision=high)
    return (inverse, jnp.dot(middle, inverse.T, precision=high))


def body(trial_block, response_weight):
    high = lax.Precision.HIGHEST
    source = response_weight[None] * trial_block
    solution = jnp.zeros_like(source)
    residual = source
    image = operate(residual)
    norm_now, product = two_products(residual, image)
    alpha = norm_now / product
    direction, along = (residual, image)
    for step in range(ITERS):
        solution = solution + expand(alpha) * direction
        residual = residual - expand(alpha) * along
        if step + 1 < ITERS:
            image = operate(residual)
            norm_next, product = two_products(residual, image)
            ratio = norm_next / norm_now
            alpha = norm_next / (product - ratio * norm_next / alpha)
            direction = residual + expand(ratio) * direction
            along = image + expand(ratio) * along
            norm_now = norm_next
    local_count = trial_block.shape[0]
    whole_x, whole_p = (
        lax.all_gather(trial_block, "vec", axis=0, tiled=True),
        lax.all_gather(solution, "vec", axis=0, tiled=True),
    )
    flat_x = whole_x.reshape(whole_x.shape[0], -1)
    flat_p = whole_p.reshape(whole_p.shape[0], -1)
    gram, cross = lax.psum(
        (jnp.dot(flat_x, flat_x.T, precision=high), jnp.dot(flat_x, flat_p.T, precision=high)),
        "grid",
    )
    cells = lax.axis_size("grid") * flat_x.shape[1]
    inverse, ritz_matrix = finish(gram, cross, cells)
    own_rows = lax.dynamic_slice_in_dim(
        inverse, lax.axis_index("vec") * local_count, local_count, 0
    )
    rotated = jnp.dot(own_rows, flat_x, precision=high).reshape(trial_block.shape)
    potentials = jnp.dot(own_rows, flat_p, precision=high).reshape(trial_block.shape)
    return (rotated, potentials, ritz_matrix)


def solution(mesh):
    placed = (P("vec", "grid", None, None), P("grid", None, None))
    return jax.shard_map(
        body,
        mesh=mesh,
        in_specs=placed,
        out_specs=(P("vec", "grid", None, None), P("vec", "grid", None, None), P()),
        check_vma=False,
    )
```

profile of v0, /device:TPU:0, one launch (start us, length us, event | category | flops | bytes accessed | tf_op | source)
XLA Modules:
  0.0 209.4 jit_solution(9174139317517877689)
XLA Ops:
  7.2 0.0 copy-start.3
  7.2 0.0 copy-start.5
  7.2 0.0 all-gather.3.cloned.1.call-start
  7.2 1.1 broadcast_multiply_fusion
  8.3 5.1 %collective-permute-start = (f32[4,6,32,128]{3,2,1,0:T(8,128)S(1)}, f32[4,6,32,128]{3,2,1,0:T(8,128)S(1)}, u32[]{:S(2)}, u32[]{:S(2)}) collective-permute-start(f32[4,6,32,128]{3,2,1,0:T(8,128)S(1)} %broadcast_multiply_fusion), channel_id=1, source_target_pairs={{0,24},{4,28},{8,0},{12,4},{16,8},{20,12},{24,16},{28,20},{1,25},{... | collective-permute-start | bytes 1179656 | tf_op jit(solution)/shard_map/ppermute | solution.py:23
  13.5 0.0 collective-permute-start.1
  13.5 4.8 %collective-permute-start.2 = (f32[4,6,6,128]{3,2,1,0:T(8,128)S(1)}, f32[4,6,6,128]{3,2,1,0:T(8,128)S(1)}, u32[]{:S(2)}, u32[]{:S(2)}) collective-permute-start(f32[4,6,6,128]{3,2,1,0:T(8,128)S(1)} %get-tuple-element.37), channel_id=1, source_target_pairs={{4,0},{8,4},{12,8},{16,12},{20,16},{24,20},{28,24},{0,28},{5,1},{9... | collective-permute-start | bytes 221192 | tf_op jit(solution)/shard_map/ppermute | solution.py:35
  18.3 0.0 collective-permute-start.3
  18.3 14.1 %collective-permute-done.2 = f32[4,6,6,128]{3,2,1,0:T(8,128)S(1)} collective-permute-done((f32[4,6,6,128]{3,2,1,0:T(8,128)S(1)}, f32[4,6,6,128]{3,2,1,0:T(8,128)S(1)}, u32[]{:S(2)}, u32[]{:S(2)}) %collective-permute-start.2) | collective-permute-done | bytes 73760 | tf_op jit(solution)/shard_map/ppermute | solution.py:35
  32.4 1.8 collective-permute-done.3
  34.2 0.0 collective-permute-done
  34.2 0.0 collective-permute-done.1
  34.2 1.8 multiply_reduce_fusion.3
  36.0 20.5 %all-reduce.6 = (f32[4]{0:T(128)S(1)}, f32[4]{0:T(128)S(1)}) all-reduce(f32[4]{0:T(128)S(1)} %get-tuple-element.15, f32[4]{0:T(128)S(1)} %get-tuple-element.14), channel_id=1, replica_groups=mesh['grid'=8,'vec'=4] {'grid'}, use_global_device_ids=true, to_apply=%region_4.5 | all-reduce | flops 8 | bytes 64 | tf_op jit(solution)/shard_map/psum | solution.py:75
  56.5 0.1 multiply_subtract_fusion.1
  56.7 0.1 collective-permute-start.4
  56.7 2.0 collective-permute-start.5
  58.8 1.5 collective-permute-start.6
  60.3 0.5 collective-permute-start.7
  60.9 0.0 all-gather.3.cloned.1.call-update
  60.9 0.0 all-gather.5.cloned.1.call-start
  60.9 10.3 %collective-permute-done.6 = f32[4,6,6,128]{3,2,1,0:T(8,128)S(1)} collective-permute-done((f32[4,6,6,128]{3,2,1,0:T(8,128)S(1)}, f32[4,6,6,128]{3,2,1,0:T(8,128)S(1)}, u32[]{:S(2)}, u32[]{:S(2)}) %collective-permute-start.6) | collective-permute-done | bytes 73760 | tf_op jit(solution)/shard_map/ppermute | solution.py:35
  71.3 0.3 collective-permute-done.7
  71.6 0.7 collective-permute-done.4
  72.3 0.0 collective-permute-done.5
  72.3 1.7 multiply_reduce_fusion.1
  74.1 21.6 %all-reduce.5 = (f32[4]{0:T(128)S(1)}, f32[4]{0:T(128)S(1)}) all-reduce(f32[4]{0:T(128)S(1)} %get-tuple-element.13, f32[4]{0:T(128)S(1)} %get-tuple-element.12), channel_id=1, replica_groups=mesh['grid'=8,'vec'=4] {'grid'}, use_global_device_ids=true, to_apply=%region_8.9 | all-reduce | flops 8 | bytes 64 | tf_op jit(solution)/shard_map/psum | solution.py:75
  95.7 0.2 multiply_reduce_fusion
  96.0 0.0 collective-permute-start.8
  96.0 2.0 collective-permute-start.9
  98.1 1.5 collective-permute-start.10
  99.5 0.6 collective-permute-start.11
  100.1 6.6 %collective-permute-done.10 = f32[4,6,6,128]{3,2,1,0:T(8,128)S(1)} collective-permute-done((f32[4,6,6,128]{3,2,1,0:T(8,128)S(1)}, f32[4,6,6,128]{3,2,1,0:T(8,128)S(1)}, u32[]{:S(2)}, u32[]{:S(2)}) %collective-permute-start.10) | collective-permute-done | bytes 73760 | tf_op jit(solution)/shard_map/ppermute | solution.py:35
  106.7 0.2 collective-permute-done.11
  107.0 1.1 collective-permute-done.8
  108.1 0.0 collective-permute-done.9
  108.1 1.7 fusion.231
  109.8 20.9 %all-reduce.4 = (f32[4]{0:T(128)S(1)}, f32[4]{0:T(128)S(1)}) all-reduce(f32[4]{0:T(128)S(1)} %get-tuple-element.26, f32[4]{0:T(128)S(1)} %fusion.231), channel_id=1, replica_groups=mesh['grid'=8,'vec'=4] {'grid'}, use_global_device_ids=true, to_apply=%region_12.13 | all-reduce | flops 8 | bytes 64 | tf_op jit(solution)/shard_map/psum | solution.py:75
  130.8 1.0 multiply_add_fusion
  131.7 0.0 all-gather.5.cloned.1.call-update
  131.7 0.0 all-gather.3.cloned.1.call-done
  131.8 2.3 %copy.64 = f32[2,8,192,128]{3,1,2,0:T(8,128)S(1)} copy(f32[2,8,192,128]{3,2,1,0:T(8,128)} %bitcast.56) | data formatting | bytes 3145728
  134.1 1.4 copy.42
  135.6 0.5 copy-done
  136.0 2.7 %fusion.9 = f32[16,16]{0,1:T(8,128)S(1)} fusion(f32[16,6,32,128]{3,2,1,0:T(8,128)S(1)} %copy-done), kind=kOutput, calls=%fused_computation.125 | convolution fusion | flops 75497472 | bytes 1573888 | tf_op jit(solution)/shard_map/dot_general | solution.py:118
  138.8 10.0 %all-gather.5.cloned.1.call-done = f32[16,6,32,128]{3,2,1,0:T(8,128)} async-done(((f32[4,6,32,128]{3,2,1,0:T(8,128)}), f32[16,6,32,128]{3,2,1,0:T(8,128)}) %all-gather.5.cloned.1.call-update) | async-done | bytes 1572880 | tf_op jit(solution)/shard_map/all_gather | solution.py:113
  148.8 5.1 %fusion.12 = f32[16,16]{0,1:T(8,128)S(1)} fusion(f32[16,6,32,128]{3,2,1,0:T(8,128)S(1)} %copy-done, f32[16,6,32,128]{3,2,1,0:T(8,128)} %all-gather.5.cloned.1.call-done), kind=kOutput, calls=%fused_computation.126 | convolution fusion | flops 75497472 | bytes 3146752 | tf_op jit(solution)/shard_map/dot_general | solution.py:118
  153.8 37.1 %all-reduce.3 = (f32[16,16]{0,1:T(8,128)S(1)}, f32[16,16]{0,1:T(8,128)S(1)}) all-reduce(f32[16,16]{0,1:T(8,128)S(1)} %fusion.9, f32[16,16]{0,1:T(8,128)S(1)} %fusion.12), channel_id=1, replica_groups=mesh['grid'=8,'vec'=4] {'grid'}, use_global_device_ids=true, to_apply=%region_0.1 | all-reduce | flops 512 | bytes 4096 | tf_op jit(solution)/shard_map/psum | solution.py:117
  191.0 0.1 copy.28
  191.0 0.1 copy.29
  191.1 1.5 cholesky.17
  192.6 0.6 compare_reduce_fusion
  193.3 0.6 fusion.232
  193.9 1.2 custom-call.6
  195.1 0.2 fusion.236
  195.3 0.1 copy.34
  195.4 0.1 fusion.234
  195.5 0.7 fusion.252
  196.3 0.9 copy.63
  197.2 0.3 copy.44
  197.5 1.7 fusion.2
  199.3 0.8 copy.36
  200.1 1.7 fusion.4
  201.8 0.8 copy.35
  (19 shorter events, 0.1 us)
Async XLA Ops:
  7.2 49.4 %copy-start.3 = (f32[4,6,32,128]{3,2,1,0:T(8,128)S(1)}, f32[4,6,32,128]{3,2,1,0:T(8,128)}, u32[]{:S(2)}) copy-start(f32[4,6,32,128]{3,2,1,0:T(8,128)} %param.2) | copy-start | bytes 1179652
  7.2 49.4 %copy-start.5 = (f32[6,32,128]{2,1,0:T(8,128)S(1)}, f32[6,32,128]{2,1,0:T(8,128)}, u32[]{:S(2)}) copy-start(f32[6,32,128]{2,1,0:T(8,128)} %param.3) | copy-start | bytes 294916
  7.2 124.6 %all-gather.3.cloned.1.call-start = ((), (), s32[]{:S(2)}) async-start(), calls=%async_computation | async-start | bytes 1966080 | tf_op jit(solution)/shard_map/all_gather | solution.py:112
  8.3 25.9 %collective-permute-start = (f32[4,6,32,128]{3,2,1,0:T(8,128)S(1)}, f32[4,6,32,128]{3,2,1,0:T(8,128)S(1)}, u32[]{:S(2)}, u32[]{:S(2)}) collective-permute-start(f32[4,6,32,128]{3,2,1,0:T(8,128)S(1)} %broadcast_multiply_fusion), channel_id=1, source_target_pairs={{0,24},{4,28},{8,0},{12,4},{16,8},{20,12},{24,16},{28,20},{1,25},{... | collective-permute-start | bytes 1179656 | tf_op jit(solution)/shard_map/ppermute | solution.py:23
  13.5 20.8 %collective-permute-start.1 = (f32[4,6,32,128]{3,2,1,0:T(8,128)S(1)}, f32[4,6,32,128]{3,2,1,0:T(8,128)S(1)}, u32[]{:S(2)}, u32[]{:S(2)}) collective-permute-start(f32[4,6,32,128]{3,2,1,0:T(8,128)S(1)} %broadcast_multiply_fusion), channel_id=1, source_target_pairs={{0,8},{4,12},{8,16},{12,20},{16,24},{20,28},{24,0},{28,4},{1,9},{5... | collective-permute-start | bytes 1179656 | tf_op jit(solution)/shard_map/ppermute | solution.py:23
  13.5 18.9 %collective-permute-start.2 = (f32[4,6,6,128]{3,2,1,0:T(8,128)S(1)}, f32[4,6,6,128]{3,2,1,0:T(8,128)S(1)}, u32[]{:S(2)}, u32[]{:S(2)}) collective-permute-start(f32[4,6,6,128]{3,2,1,0:T(8,128)S(1)} %get-tuple-element.37), channel_id=1, source_target_pairs={{4,0},{8,4},{12,8},{16,12},{20,16},{24,20},{28,24},{0,28},{5,1},{9... | collective-permute-start | bytes 221192 | tf_op jit(solution)/shard_map/ppermute | solution.py:35
  18.3 15.9 %collective-permute-start.3 = (f32[4,6,6,128]{3,2,1,0:T(8,128)S(1)}, f32[4,6,6,128]{3,2,1,0:T(8,128)S(1)}, u32[]{:S(2)}, u32[]{:S(2)}) collective-permute-start(f32[4,6,6,128]{3,2,1,0:T(8,128)S(1)} %get-tuple-element.38), channel_id=1, source_target_pairs={{0,4},{4,8},{8,12},{12,16},{16,20},{20,24},{24,28},{28,0},{1,5},{5... | collective-permute-start | bytes 221192 | tf_op jit(solution)/shard_map/ppermute | solution.py:33
  56.7 15.7 %collective-permute-start.4 = (f32[4,6,32,128]{3,2,1,0:T(8,128)S(1)}, f32[4,6,32,128]{3,2,1,0:T(8,128)S(1)}, u32[]{:S(2)}, u32[]{:S(2)}) collective-permute-start(f32[4,6,32,128]{3,2,1,0:T(8,128)S(1)} %multiply_subtract_fusion.1), channel_id=1, source_target_pairs={{0,24},{4,28},{8,0},{12,4},{16,8},{20,12},{24,16},{28,20},{1,25},{... | collective-permute-start | bytes 1179656 | tf_op jit(solution)/shard_map/ppermute | solution.py:23
  56.7 15.6 %collective-permute-start.5 = (f32[4,6,32,128]{3,2,1,0:T(8,128)S(1)}, f32[4,6,32,128]{3,2,1,0:T(8,128)S(1)}, u32[]{:S(2)}, u32[]{:S(2)}) collective-permute-start(f32[4,6,32,128]{3,2,1,0:T(8,128)S(1)} %multiply_subtract_fusion.1), channel_id=1, source_target_pairs={{0,8},{4,12},{8,16},{12,20},{16,24},{20,28},{24,0},{28,4},{1,9},{5... | collective-permute-start | bytes 1179656 | tf_op jit(solution)/shard_map/ppermute | solution.py:23
  58.8 12.5 %collective-permute-start.6 = (f32[4,6,6,128]{3,2,1,0:T(8,128)S(1)}, f32[4,6,6,128]{3,2,1,0:T(8,128)S(1)}, u32[]{:S(2)}, u32[]{:S(2)}) collective-permute-start(f32[4,6,6,128]{3,2,1,0:T(8,128)S(1)} %get-tuple-element.35), channel_id=1, source_target_pairs={{4,0},{8,4},{12,8},{16,12},{20,16},{24,20},{28,24},{0,28},{5,1},{9... | collective-permute-start | bytes 221192 | tf_op jit(solution)/shard_map/ppermute | solution.py:35
  60.3 11.3 %collective-permute-start.7 = (f32[4,6,6,128]{3,2,1,0:T(8,128)S(1)}, f32[4,6,6,128]{3,2,1,0:T(8,128)S(1)}, u32[]{:S(2)}, u32[]{:S(2)}) collective-permute-start(f32[4,6,6,128]{3,2,1,0:T(8,128)S(1)} %get-tuple-element.36), channel_id=1, source_target_pairs={{0,4},{4,8},{8,12},{12,16},{16,20},{20,24},{24,28},{28,0},{1,5},{5... | collective-permute-start | bytes 221192 | tf_op jit(solution)/shard_map/ppermute | solution.py:33
  60.9 87.9 %all-gather.5.cloned.1.call-start = ((), (), s32[]{:S(2)}) async-start(), calls=%async_computation.1 | async-start | bytes 1966080 | tf_op jit(solution)/shard_map/all_gather | solution.py:113
  95.7 35.0 %copy-start.4 = (f32[4,6,32,128]{3,2,1,0:T(8,128)S(1)}, f32[4,6,32,128]{3,2,1,0:T(8,128)}, u32[]{:S(2)}) copy-start(f32[4,6,32,128]{3,2,1,0:T(8,128)} %param.2) | copy-start | bytes 1179652
  96.0 12.1 %collective-permute-start.8 = (f32[4,6,32,128]{3,2,1,0:T(8,128)S(1)}, f32[4,6,32,128]{3,2,1,0:T(8,128)S(1)}, u32[]{:S(2)}, u32[]{:S(2)}) collective-permute-start(f32[4,6,32,128]{3,2,1,0:T(8,128)S(1)} %get-tuple-element.27), channel_id=1, source_target_pairs={{0,24},{4,28},{8,0},{12,4},{16,8},{20,12},{24,16},{28,20},{1,25},{... | collective-permute-start | bytes 1179656 | tf_op jit(solution)/shard_map/ppermute | solution.py:23
  96.0 12.1 %collective-permute-start.9 = (f32[4,6,32,128]{3,2,1,0:T(8,128)S(1)}, f32[4,6,32,128]{3,2,1,0:T(8,128)S(1)}, u32[]{:S(2)}, u32[]{:S(2)}) collective-permute-start(f32[4,6,32,128]{3,2,1,0:T(8,128)S(1)} %get-tuple-element.27), channel_id=1, source_target_pairs={{0,8},{4,12},{8,16},{12,20},{16,24},{20,28},{24,0},{28,4},{1,9},{5... | collective-permute-start | bytes 1179656 | tf_op jit(solution)/shard_map/ppermute | solution.py:23
  98.1 8.7 %collective-permute-start.10 = (f32[4,6,6,128]{3,2,1,0:T(8,128)S(1)}, f32[4,6,6,128]{3,2,1,0:T(8,128)S(1)}, u32[]{:S(2)}, u32[]{:S(2)}) collective-permute-start(f32[4,6,6,128]{3,2,1,0:T(8,128)S(1)} %get-tuple-element.33), channel_id=1, source_target_pairs={{4,0},{8,4},{12,8},{16,12},{20,16},{24,20},{28,24},{0,28},{5,1},{9... | collective-permute-start | bytes 221192 | tf_op jit(solution)/shard_map/ppermute | solution.py:35
  99.5 7.4 %collective-permute-start.11 = (f32[4,6,6,128]{3,2,1,0:T(8,128)S(1)}, f32[4,6,6,128]{3,2,1,0:T(8,128)S(1)}, u32[]{:S(2)}, u32[]{:S(2)}) collective-permute-start(f32[4,6,6,128]{3,2,1,0:T(8,128)S(1)} %get-tuple-element.34), channel_id=1, source_target_pairs={{0,4},{4,8},{8,12},{12,16},{16,20},{20,24},{24,28},{28,0},{1,5},{5... | collective-permute-start | bytes 221192 | tf_op jit(solution)/shard_map/ppermute | solution.py:33
  134.1 1.9 copy-start
  148.8 47.5 %copy-start.1 = (f32[16,6,32,128]{3,2,1,0:T(8,128)S(1)}, f32[16,6,32,128]{3,2,1,0:T(8,128)}, u32[]{:S(2)}) copy-start(f32[16,6,32,128]{3,2,1,0:T(8,128)} %all-gather.5.cloned.1.call-done) | copy-start | bytes 4718596
  197.5 2.5 %copy-start.2 = (f32[2,8,192,128]{3,2,1,0:T(8,128)S(1)}, f32[2,8,192,128]{3,2,1,0:T(8,128)}, u32[]{:S(2)}) copy-start(f32[2,8,192,128]{3,2,1,0:T(8,128)} %copy.42) | copy-start | bytes 4718596
Sparse Core Ops, SparseCore 0:
  61.0 20.5 all-gather.2
  131.9 16.8 all-gather.4
where the time goes:
time: 210 us; the launch traced here: 209 us
  blocking collectives  100 us (48%)
  waiting for transfers between devices  45.3 us (22%)
  starting transfers between devices  18.3 us (9%)
  between operations  14.2 us (7%)
  matrix products  12.3 us (6%)
  other arithmetic  11.7 us (6%)
  local copies, waits for them, and re-layouts  7.35 us (4%)
    psum x3, blocking collectives, two_products(): return lax.psum((inner(residual, residual), inner(residual, image)), 'grid')  63.1 us
    psum x1, blocking collectives, body(): lax.psum((jnp.dot(flat_x, flat_x.T, precision=high), jnp.dot(flat_x, flat...  37.1 us
    ppermute x3, waiting for transfers between devices, with_halo(): lax.ppermute(head, axis, [((i + 1) % count, i) for i in range(count)])  31 us
    all_gather x1, waiting for transfers between devices, body(): lax.all_gather(solution, 'vec', axis=0, tiled=True)  10 us
    ppermute x6, starting transfers between devices, shifted(): return lax.ppermute(value, axis, pairs)  9.25 us
    ppermute x3, starting transfers between devices, with_halo(): lax.ppermute(head, axis, [((i + 1) % count, i) for i in range(count)])  7.84 us
    unnamed x18, local copies, waits for them, and re-layouts  7.09 us
    reduce_sum x4, other arithmetic, inner(): return jnp.sum(left * right, axis=(1, 2, 3))  5.46 us
  transfers between devices with their start and end apart: 14, of which 9 were waited for; matrix products, arithmetic and copies ran while one was open for 5% of the time, Pallas kernels for 0%

commit v1 on v0

--- a/solution.py
+++ b/solution.py
@@ -1,6 +1,10 @@
+import functools
+
 import jax
 import jax.numpy as jnp
 from jax import lax
+from jax.experimental import pallas as pl
+from jax.experimental.pallas import tpu as pltpu
 from jax.sharding import PartitionSpec as P
 
 ITERS = 3
@@ -128,10 +132,421 @@
     return (rotated, potentials, ritz_matrix)
 
 
+MESH_ID = pl.DeviceIdType.MESH
+PAD = 8
+HALO = 6
+
+
+def kernel(
+    groups, parts, trial, weight, rotated, potentials, ritz,
+    src, pad, img, dirn, along, phi, sums, sums_in, held, waves, gmsg, gin, cmsg, cin, mats, coef,
+    fsend, frecv, hsend, hrecv, ssend, srecv, tsend, trecv, rsend, rrecv,
+    bsend, brecv, psend, precv, xsend, xrecv, ysend, yrecv, gsend, grecv, csend, crecv,
+):
+    nl, rows, cols, depth = trial.shape
+    nvec = parts * nl
+    length = pad.shape[0]
+    blocks = length // rows
+    pairs = parts // 2
+    total_devices = groups * parts
+    me_g = lax.axis_index("grid")
+    me_v = lax.axis_index("vec")
+    me = me_g * parts + me_v
+    pair = lax.div(me_v, 2)
+    core = lax.rem(me_v, 2)
+    partner = (me_g, pair * 2 + 1 - core)
+    blk = lax.div(me_g, 2)
+    half = lax.rem(me_g, 2)
+    center = slice(PAD, PAD + cols)
+
+    barrier = pltpu.get_barrier_semaphore()
+
+    def device_at(k):
+        target = lax.rem(me + k, total_devices)
+        return (lax.div(target, parts), lax.rem(target, parts))
+
+    def greet(k, carry):
+        pl.semaphore_signal(barrier, inc=1, device_id=device_at(k), device_id_type=MESH_ID)
+        return carry
+
+    lax.fori_loop(1, total_devices, greet, 0)
+
+    def prepare(i, carry):
+        scale = weight[i]
+        for s in range(nl):
+            value = trial[s, i]
+            src[s, i] = scale * value
+            held[me_v * nl + s, i] = value
+        return carry
+
+    lax.fori_loop(0, rows, prepare, 0)
+    pl.semaphore_wait(barrier, total_devices - 1)
+
+    def remote(source, target, send, recv, device):
+        return pltpu.make_async_remote_copy(
+            src_ref=source, dst_ref=target, send_sem=send, recv_sem=recv,
+            device_id=device, device_id_type=MESH_ID,
+        )
+
+    def forward(s):
+        return remote(
+            src.at[s], pad.at[pl.ds(blk * rows, rows), center], fsend.at[s], frecv.at[blk],
+            (core * nl + s, pair * 2 + half),
+        )
+
+    def own_slot(s):
+        return jnp.logical_and(core * nl + s == me_g, half == core)
+
+    for step in range(nl):
+        s = lax.rem(me_g + step, nl)
+
+        @pl.when(jnp.logical_not(own_slot(s)))
+        def _():
+            forward(s).start()
+
+        @pl.when(own_slot(s))
+        def _():
+            pad[pl.ds(blk * rows, rows), center] = src[s]
+
+    def slot_ref(buffer, v):
+        return buffer.at[pl.ds(v * nl, nl)]
+
+    def trial_copy(q):
+        device = partner if q == 0 else (me_g, lax.rem(pair + q, pairs) * 2 + core)
+        return remote(trial, slot_ref(held, me_v), tsend.at[q], trecv.at[q], device)
+
+    def from_pair(q):
+        return lax.rem(pair - q + pairs, pairs) * 2 + core
+
+    def trial_relay(q):
+        v = from_pair(q)
+        return remote(slot_ref(held, v), slot_ref(held, v), rsend.at[q], rrecv.at[q], partner)
+
+    for q in list(range(1, pairs)) + [0]:
+        trial_copy(q).start()
+
+    owner_v = pair * 2 + lax.div(me_g, nl)
+    for bx in range(blocks):
+        @pl.when(jnp.logical_not(jnp.logical_and(bx * 2 + core == me_g, owner_v == me_v)))
+        def _():
+            remote(
+                src.at[0], pad.at[pl.ds(bx * rows, rows), center], fsend.at[0], frecv.at[bx], partner
+            ).wait_recv()
+
+    lane = lax.broadcasted_iota(jnp.int32, (cols, depth), 1)
+
+    def halo(side, bx):
+        if side == 0:
+            shift, here, there = core, slice(cols, PAD + cols), slice(0, PAD)
+        else:
+            shift, here, there = core - 1, slice(PAD, 2 * PAD), slice(PAD + cols, 2 * PAD + cols)
+        target = lax.rem(bx + shift + blocks, blocks)
+        return remote(
+            pad.at[pl.ds(bx * rows, rows), here], pad.at[pl.ds(target * rows, rows), there],
+            hsend.at[side, bx], hrecv.at[side, bx], partner,
+        )
+
+    halos = [(side, bx) for bx in range(blocks) for side in range(2)]
+
+    def pass_xz(x, carry):
+        value = pad[x, center]
+        acc = (3.0 * COEFFS[0]) * value
+        for k in range(1, HALO + 1):
+            near = pad[lax.rem(x + k, length), center] + pad[lax.rem(x + length - k, length), center]
+            up = jnp.where(lane < depth - k, pltpu.roll(value, depth - k, 1), 0.0)
+            low = jnp.where(lane >= k, pltpu.roll(value, k, 1), 0.0)
+            acc = acc + COEFFS[k] * (near + (up + low))
+        img[x] = acc
+        return carry
+
+    def pass_y(x, carry):
+        norm, product = carry
+        acc = img[x]
+        for k in range(1, HALO + 1):
+            acc = acc + COEFFS[k] * (
+                pad[x, PAD + k : PAD + k + cols] + pad[x, PAD - k : PAD - k + cols]
+            )
+        acc = -acc
+        img[x] = acc
+        value = pad[x, center]
+        return (norm + value * value, product + value * acc)
+
+    def folded(value):
+        return value.reshape(cols // 8, 8, depth).sum(axis=0)
+
+    def back(bx):
+        return remote(
+            phi.at[pl.ds(bx * rows, rows)], waves.at[pair * 2 * nl + me_g],
+            bsend.at[bx], brecv.at[lax.rem(me_g, nl)], (bx * 2 + core, owner_v),
+        )
+
+    norm_now = alpha = None
+    for step in range(ITERS):
+        for side, bx in halos:
+            halo(side, bx).start()
+        lax.fori_loop(0, length, pass_xz, 0, unroll=2)
+        for side, bx in halos:
+            halo(side, bx).wait_recv()
+        zero = jnp.zeros((cols, depth), jnp.float32)
+        norm, product = lax.fori_loop(0, length, pass_y, (zero, zero), unroll=2)
+        sums[step, 0] = folded(norm)
+        sums[step, 1] = folded(product)
+        exchange = remote(sums.at[step], sums_in.at[step], ssend.at[step], srecv.at[step], partner)
+        exchange.start()
+        for side, bx in halos:
+            halo(side, bx).wait_send()
+        if step == 0:
+            for q in range(1, pairs):
+                trial_copy(q).wait_recv()
+                trial_relay(q).start()
+        exchange.wait()
+        norm_next = jnp.sum(sums[step, 0] + sums_in[step, 0], axis=(0, 1), keepdims=True)
+        product = jnp.sum(sums[step, 1] + sums_in[step, 1], axis=(0, 1), keepdims=True)
+        last = step + 1 == ITERS
+        if step == 0:
+            alpha = norm_next / product
+            ratio = None
+        else:
+            ratio = norm_next / norm_now
+            alpha = norm_next / (product - ratio * norm_next / alpha)
+            ratio_wide = jnp.broadcast_to(ratio, (cols, depth))
+        norm_now = norm_next
+        alpha_wide = jnp.broadcast_to(alpha, (cols, depth))
+
+        def update(x, carry):
+            value = pad[x, center]
+            image = img[x]
+            if step == 0:
+                phi[x] = alpha_wide * value
+                dirn[x] = value
+                along[x] = image
+            else:
+                value_dir = value + ratio_wide * dirn[x]
+                phi[x] = phi[x] + alpha_wide * value_dir
+                if not last:
+                    dirn[x] = value_dir
+                    image = image + ratio_wide * along[x]
+                    along[x] = image
+            if not last:
+                pad[x, center] = value - alpha_wide * image
+            return carry
+
+        if not last:
+            lax.fori_loop(0, length, update, 0, unroll=2)
+        else:
+            for bx in range(blocks):
+                lax.fori_loop(bx * rows, (bx + 1) * rows, update, 0, unroll=2)
+                own = jnp.logical_and(bx * 2 + core == me_g, owner_v == me_v)
+
+                @pl.when(jnp.logical_not(own))
+                def _():
+                    back(bx).start()
+
+                @pl.when(own)
+                def _():
+                    waves[pair * 2 * nl + me_g] = phi[bx * rows : (bx + 1) * rows]
+
+    lane_row = lax.broadcasted_iota(jnp.int32, (nl, depth), 1)
+
+    def products(buffer):
+        def one(j, acc):
+            other = held[j]
+            parts_of = [
+                jnp.sum(jnp.sum(buffer[me_v * nl + s] * other, axis=0), axis=0, keepdims=True)
+                for s in range(nl)
+            ]
+            value = jnp.sum(jnp.concatenate(parts_of, axis=0), axis=1, keepdims=True)
+            return jnp.where(lane_row == j, value, acc)
+
+        return lax.fori_loop(0, nvec, one, jnp.zeros((nl, depth), jnp.float32), unroll=4)
+
+    def spread(message, inbox, send, recv):
+        inbox[me_g, me_v] = message[...]
+
+        def start(k, carry):
+            remote(message, inbox.at[me_g, me_v], send.at[k], recv.at[me], device_at(k)).start()
+            return carry
+
+        lax.fori_loop(1, total_devices, start, 0)
+
+    def collect(message, inbox, send, recv, slot):
+        def wait(k, carry):
+            g, v = device_at(k)
+            copy = remote(message, inbox.at[g, v], send.at[k], recv.at[g * parts + v], (g, v))
+            copy.wait_recv()
+            copy.wait_send()
+            return carry
+
+        lax.fori_loop(1, total_devices, wait, 0)
+        for v in range(parts):
+            total = inbox[0, v]
+            for g in range(1, groups):
+                total = total + inbox[g, v]
+            mats[slot, v * nl : (v + 1) * nl] = total / (groups * rows * cols * depth)
+
+    trial_copy(0).wait_recv()
+    for q in range(1, pairs):
+        trial_relay(q).wait_recv()
+    gmsg[...] = products(held)
+    spread(gmsg, gin, gsend, grecv)
+
+    def wave_core(s):
+        slot = waves.at[me_v * nl + s]
+        return remote(slot, slot, psend.at[s], precv.at[s], partner)
+
+    def wave_over(q, s):
+        slot = waves.at[me_v * nl + s]
+        return remote(
+            slot, slot, xsend.at[q, s], xrecv.at[q, s], (me_g, lax.rem(pair + q, pairs) * 2 + core)
+        )
+
+    def wave_from(q, s):
+        slot = waves.at[from_pair(q) * nl + s]
+        return remote(slot, slot, xsend.at[q, s], xrecv.at[q, s], partner)
+
+    def wave_relay(q, s):
+        slot = waves.at[from_pair(q) * nl + s]
+        return remote(slot, slot, ysend.at[q, s], yrecv.at[q, s], partner)
+
+    for s in range(nl):
+        @pl.when(jnp.logical_not(own_slot(s)))
+        def _():
+            slot = waves.at[me_v * nl + s]
+            remote(phi.at[0:rows], slot, bsend.at[0], brecv.at[s], partner).wait_recv()
+
+        for q in range(1, pairs):
+            wave_over(q, s).start()
+        wave_core(s).start()
+
+    cmsg[...] = products(waves)
+    spread(cmsg, cin, csend, crecv)
+    for q in range(1, pairs):
+        for s in range(nl):
+            wave_from(q, s).wait_recv()
+            wave_relay(q, s).start()
+
+    collect(gmsg, gin, gsend, grecv, 0)
+    gram = mats[0]
+    row_of = lax.broadcasted_iota(jnp.int32, (nvec, depth), 0)
+    lane_of = lax.broadcasted_iota(jnp.int32, (nvec, depth), 1)
+    inverse = jnp.where(row_of == lane_of, 1.0, 0.0)
+    for k in range(nvec):
+        scale = 1.0 / jnp.sqrt(gram[k : k + 1, k : k + 1])
+        column = gram[:, k : k + 1] * scale
+        line = inverse[k : k + 1] * scale
+        inverse = jnp.where(row_of > k, inverse - column * line, jnp.where(row_of == k, line, inverse))
+        gram = gram - column * (gram[k : k + 1] * scale)
+    mats[1] = inverse
+    own_rows = mats[1, pl.ds(me_v * nl, nl)]
+    for i in range(nvec):
+        coef[i] = jnp.broadcast_to(own_rows[:, i : i + 1], (nl, depth))
+
+    def rotate(buffer, out):
+        def one(row, carry):
+            totals = [None] * nl
+            for i in range(nvec):
+                value = buffer[i, row]
+                for s in range(nl):
+                    term = coef[i, s : s + 1] * value
+                    totals[s] = term if i == 0 else totals[s] + term
+            for s in range(nl):
+                out[s, row] = totals[s]
+            return carry
+
+        lax.fori_loop(0, rows, one, 0)
+
+    rotate(held, rotated)
+    for s in range(nl):
+        slot = waves.at[(pair * 2 + 1 - core) * nl + s]
+        remote(slot, slot, psend.at[s], precv.at[s], partner).wait_recv()
+    for q in range(1, pairs):
+        for s in range(nl):
+            wave_relay(q, s).wait_recv()
+    rotate(waves, potentials)
+
+    collect(cmsg, cin, csend, crecv, 2)
+    cross = mats[2]
+    high = lax.Precision.HIGHEST
+    last_dims = (((1,), (1,)), ((), ()))
+    inverse = mats[1]
+    small = inverse[:, :nvec]
+    middle = 0.5 * (
+        jnp.dot(small, cross, precision=high)[:, :nvec]
+        + lax.dot_general(inverse, cross, last_dims, precision=high)
+    )
+    ritz[...] = lax.dot_general(middle, small, last_dims, precision=high)
+
+    for s in range(nl):
+        @pl.when(jnp.logical_not(own_slot(s)))
+        def _():
+            forward(s).wait_send()
+
+        wave_core(s).wait_send()
+    for bx in range(blocks):
+        @pl.when(jnp.logical_not(jnp.logical_and(bx * 2 + core == me_g, owner_v == me_v)))
+        def _():
+            back(bx).wait_send()
+    for q in range(pairs):
+        trial_copy(q).wait_send()
+    for q in range(1, pairs):
+        trial_relay(q).wait_send()
+        for s in range(nl):
+            wave_over(q, s).wait_send()
+            wave_relay(q, s).wait_send()
+
+
+def paired_body(trial_block, response_weight):
+    nl, rows, cols, depth = trial_block.shape
+    groups, parts = lax.axis_size("grid"), lax.axis_size("vec")
+    nvec, blocks = parts * nl, groups // 2
+    pairs, length, devices = parts // 2, (groups // 2) * rows, groups * parts
+    f32 = jnp.float32
+    dma = pltpu.SemaphoreType.DMA
+    vmem = pl.BlockSpec(memory_space=pltpu.VMEM)
+    field = pltpu.VMEM((length, cols, depth), f32)
+    whole = pltpu.VMEM((nvec, rows, cols, depth), f32)
+    inbox = pltpu.VMEM((groups, parts, nl, depth), f32)
+    message = pltpu.VMEM((nl, depth), f32)
+    small = pltpu.VMEM((ITERS, 2, 8, depth), f32)
+    return pl.pallas_call(
+        functools.partial(kernel, groups, parts),
+        out_shape=(
+            jax.ShapeDtypeStruct(trial_block.shape, f32),
+            jax.ShapeDtypeStruct(trial_block.shape, f32),
+            jax.ShapeDtypeStruct((nvec, nvec), f32),
+        ),
+        in_specs=[vmem, vmem],
+        out_specs=(vmem, vmem, vmem),
+        scratch_shapes=[
+            pltpu.VMEM((nl, rows, cols, depth), f32),
+            pltpu.VMEM((length, cols + 2 * PAD, depth), f32),
+            field, field, field, field, small, small, whole, whole,
+            message, inbox, message, inbox,
+            pltpu.VMEM((3, nvec, depth), f32), pltpu.VMEM((nvec, nl, depth), f32),
+            dma((nl,)), dma((blocks,)), dma((2, blocks)), dma((2, blocks)),
+            dma((ITERS,)), dma((ITERS,)), dma((pairs,)), dma((pairs,)), dma((pairs,)), dma((pairs,)),
+            dma((blocks,)), dma((nl,)), dma((nl,)), dma((nl,)),
+            dma((pairs, nl)), dma((pairs, nl)), dma((pairs, nl)), dma((pairs, nl)),
+            dma((devices,)), dma((devices,)), dma((devices,)), dma((devices,)),
+        ],
+        compiler_params=pltpu.CompilerParams(collective_id=0, has_side_effects=True),
+    )(trial_block, response_weight)
+
+
+def chosen_body(trial_block, response_weight):
+    nl, rows, cols, depth = trial_block.shape
+    groups, parts = lax.axis_size("grid"), lax.axis_size("vec")
+    fits = (
+        max(groups // 16, 2) == 2 and groups == 2 * nl and parts % 2 == 0 and rows == HALO
+        and cols % 8 == 0 and cols >= PAD and parts * nl <= depth
+    )
+    return (paired_body if fits else body)(trial_block, response_weight)
+
+
 def solution(mesh):
     placed = (P("vec", "grid", None, None), P("grid", None, None))
     return jax.shard_map(
-        body,
+        chosen_body,
         mesh=mesh,
         in_specs=placed,
         out_specs=(P("vec", "grid", None, None), P("vec", "grid", None, None), P()),

time: 210 us -> 55.5 us (0.26)
  the two profiles are of different devices: /device:TPU:0 before, /device:TPU:1 now
where the time goes in v1:
time: 55.5 us; the launch traced here: 55.3 us
  Pallas kernels  51.5 us (93%)
  local copies, waits for them, and re-layouts  3.17 us (6%)
  between operations  0.65 us (1%)
    pallas_call x1, Pallas kernels, paired_body(): pl.pallas_call(functools.partial(kernel, groups, parts), out_shape=(jax.S...  51.5 us
    unnamed x7, local copies, waits for them, and re-layouts  3.17 us

profile of v1, /device:TPU:1, one launch (start us, length us, event | category | flops | bytes accessed | tf_op | source)
XLA Modules:
  0.0 55.3 jit_solution(10258315038448154152)
XLA Ops:
  0.6 51.5 %shard_map.49 = (f32[4,6,32,128]{3,2,1,0:T(8,128)}, f32[4,6,32,128]{3,2,1,0:T(8,128)}, f32[16,16]{1,0:T(8,128)}) custom-call(f32[4,6,32,128]{3,2,1,0:T(8,128)} %trial.1, f32[6,32,128]{2,1,0:T(8,128)} %weight.1), custom_call_target="tpu_custom_call" | custom-call | tf_op jit(solution)/shard_map/pallas_call | solution.py:511
  52.1 0.0 copy-start
  52.1 1.8 %copy.8 = f32[4,6,32,128]{3,2,1,0:T(8,128)} copy(f32[4,6,32,128]{3,2,1,0:T(8,128)} %get-tuple-element.6) | data formatting | bytes 786432
  53.9 0.0 copy-done
  54.0 0.0 copy-start.1
  54.0 0.7 %copy.9 = f32[4,6,32,128]{3,2,1,0:T(8,128)} copy(f32[4,6,32,128]{3,2,1,0:T(8,128)S(1)} %copy-done) | data formatting | bytes 786432
  54.7 0.0 copy-done.1
  54.7 0.6 %copy.10 = f32[16,16]{1,0:T(8,128)} copy(f32[16,16]{1,0:T(8,128)S(1)} %copy-done.1) | data formatting | bytes 2048
Async XLA Ops:
  52.1 1.8 %copy-start = (f32[4,6,32,128]{3,2,1,0:T(8,128)S(1)}, f32[4,6,32,128]{3,2,1,0:T(8,128)}, u32[]{:S(2)}) copy-start(f32[4,6,32,128]{3,2,1,0:T(8,128)} %get-tuple-element.7) | copy-start | bytes 1179652
  54.0 0.8 %copy-start.1 = (f32[16,16]{1,0:T(8,128)S(1)}, f32[16,16]{1,0:T(8,128)}, u32[]{:S(2)}) copy-start(f32[16,16]{1,0:T(8,128)} %get-tuple-element.8) | copy-start | bytes 3076

commit v2 on v1

--- a/solution.py
+++ b/solution.py
@@ -139,9 +139,9 @@
 
 def kernel(
     groups, parts, trial, weight, rotated, potentials, ritz,
-    src, pad, img, dirn, along, phi, sums, sums_in, held, waves, gmsg, gin, cmsg, cin, mats, coef,
+    wbuf, src, pad, img, dirn, along, phi, sums, sums_in, held, waves, gmsg, gin, cmsg, cin, mats, coef,
     fsend, frecv, hsend, hrecv, ssend, srecv, tsend, trecv, rsend, rrecv,
-    bsend, brecv, psend, precv, xsend, xrecv, ysend, yrecv, gsend, grecv, csend, crecv,
+    bsend, brecv, psend, precv, xsend, xrecv, ysend, yrecv, gsend, grecv, csend, crecv, isend,
 ):
     nl, rows, cols, depth = trial.shape
     nvec = parts * nl
@@ -171,12 +171,19 @@
 
     lax.fori_loop(1, total_devices, greet, 0)
 
+    fetches = [
+        pltpu.make_async_copy(weight, wbuf, isend.at[0]),
+        pltpu.make_async_copy(trial, held.at[pl.ds(me_v * nl, nl)], isend.at[1]),
+    ]
+    for fetch in fetches:
+        fetch.start()
+    for fetch in fetches:
+        fetch.wait()
+
     def prepare(i, carry):
-        scale = weight[i]
+        scale = wbuf[i]
         for s in range(nl):
-            value = trial[s, i]
-            src[s, i] = scale * value
-            held[me_v * nl + s, i] = value
+            src[s, i] = scale * held[me_v * nl + s, i]
         return carry
 
     lax.fori_loop(0, rows, prepare, 0)
@@ -213,7 +220,7 @@
 
     def trial_copy(q):
         device = partner if q == 0 else (me_g, lax.rem(pair + q, pairs) * 2 + core)
-        return remote(trial, slot_ref(held, me_v), tsend.at[q], trecv.at[q], device)
+        return remote(slot_ref(held, me_v), slot_ref(held, me_v), tsend.at[q], trecv.at[q], device)
 
     def from_pair(q):
         return lax.rem(pair - q + pairs, pairs) * 2 + core
@@ -224,16 +231,6 @@
 
     for q in list(range(1, pairs)) + [0]:
         trial_copy(q).start()
-
-    owner_v = pair * 2 + lax.div(me_g, nl)
-    for bx in range(blocks):
-        @pl.when(jnp.logical_not(jnp.logical_and(bx * 2 + core == me_g, owner_v == me_v)))
-        def _():
-            remote(
-                src.at[0], pad.at[pl.ds(bx * rows, rows), center], fsend.at[0], frecv.at[bx], partner
-            ).wait_recv()
-
-    lane = lax.broadcasted_iota(jnp.int32, (cols, depth), 1)
 
     def halo(side, bx):
         if side == 0:
@@ -245,6 +242,19 @@
             pad.at[pl.ds(bx * rows, rows), here], pad.at[pl.ds(target * rows, rows), there],
             hsend.at[side, bx], hrecv.at[side, bx], partner,
         )
+
+    owner_v = pair * 2 + lax.div(me_g, nl)
+    for bx in range(blocks):
+        @pl.when(jnp.logical_not(jnp.logical_and(bx * 2 + core == me_g, owner_v == me_v)))
+        def _():
+            remote(
+                src.at[0], pad.at[pl.ds(bx * rows, rows), center], fsend.at[0], frecv.at[bx], partner
+            ).wait_recv()
+
+        for side in range(2):
+            halo(side, bx).start()
+
+    lane = lax.broadcasted_iota(jnp.int32, (cols, depth), 1)
 
     halos = [(side, bx) for bx in range(blocks) for side in range(2)]
 
@@ -280,15 +290,51 @@
             bsend.at[bx], brecv.at[lax.rem(me_g, nl)], (bx * 2 + core, owner_v),
         )
 
+    lane_row = lax.broadcasted_iota(jnp.int32, (nl, depth), 1)
+
+    def products(buffer, slots):
+        def one(j, acc):
+            other = held[j]
+            parts_of = [
+                jnp.sum(jnp.sum(buffer[me_v * nl + s] * other, axis=0), axis=0, keepdims=True)
+                for s in slots
+            ]
+            value = jnp.sum(jnp.concatenate(parts_of, axis=0), axis=1, keepdims=True)
+            return jnp.where(lane_row[: len(slots)] == j, value, acc)
+
+        return lax.fori_loop(0, nvec, one, jnp.zeros((len(slots), depth), jnp.float32), unroll=4)
+
+    def spread(message, inbox, send, recv):
+        inbox[me_g, me_v] = message[...]
+
+        def start(k, carry):
+            remote(message, inbox.at[me_g, me_v], send.at[k], recv.at[me], device_at(k)).start()
+            return carry
+
+        lax.fori_loop(1, total_devices, start, 0)
+
+    def collect(message, inbox, send, recv, slot):
+        def wait(k, carry):
+            g, v = device_at(k)
+            copy = remote(message, inbox.at[g, v], send.at[k], recv.at[g * parts + v], (g, v))
+            copy.wait_recv()
+            copy.wait_send()
+            return carry
+
+        lax.fori_loop(1, total_devices, wait, 0)
+        for v in range(parts):
+            total = inbox[0, v]
+            for g in range(1, groups):
+                total = total + inbox[g, v]
+            mats[slot, v * nl : (v + 1) * nl] = total / (groups * rows * cols * depth)
+
     norm_now = alpha = None
     for step in range(ITERS):
-        for side, bx in halos:
-            halo(side, bx).start()
-        lax.fori_loop(0, length, pass_xz, 0, unroll=2)
+        lax.fori_loop(0, length, pass_xz, 0, unroll=4)
         for side, bx in halos:
             halo(side, bx).wait_recv()
         zero = jnp.zeros((cols, depth), jnp.float32)
-        norm, product = lax.fori_loop(0, length, pass_y, (zero, zero), unroll=2)
+        norm, product = lax.fori_loop(0, length, pass_y, (zero, zero), unroll=4)
         sums[step, 0] = folded(norm)
         sums[step, 1] = folded(product)
         exchange = remote(sums.at[step], sums_in.at[step], ssend.at[step], srecv.at[step], partner)
@@ -299,6 +345,12 @@
             for q in range(1, pairs):
                 trial_copy(q).wait_recv()
                 trial_relay(q).start()
+        if step == 1:
+            trial_copy(0).wait_recv()
+            for q in range(1, pairs):
+                trial_relay(q).wait_recv()
+            gmsg[...] = products(held, range(nl))
+            spread(gmsg, gin, gsend, grecv)
         exchange.wait()
         norm_next = jnp.sum(sums[step, 0] + sums_in[step, 0], axis=(0, 1), keepdims=True)
         product = jnp.sum(sums[step, 1] + sums_in[step, 1], axis=(0, 1), keepdims=True)
@@ -332,10 +384,15 @@
             return carry
 
         if not last:
-            lax.fori_loop(0, length, update, 0, unroll=2)
+            for bx in range(blocks):
+                lax.fori_loop(bx * rows, (bx + 1) * rows, update, 0, unroll=rows)
+                for side in range(2):
+                    halo(side, bx).start()
         else:
             for bx in range(blocks):
-                lax.fori_loop(bx * rows, (bx + 1) * rows, update, 0, unroll=2)
+                lax.fori_loop(
+                    0, rows, lambda i, carry: update(bx * rows + i, carry), 0, unroll=rows
+                )
                 own = jnp.logical_and(bx * 2 + core == me_g, owner_v == me_v)
 
                 @pl.when(jnp.logical_not(own))
@@ -344,51 +401,7 @@
 
                 @pl.when(own)
                 def _():
-                    waves[pair * 2 * nl + me_g] = phi[bx * rows : (bx + 1) * rows]
-
-    lane_row = lax.broadcasted_iota(jnp.int32, (nl, depth), 1)
-
-    def products(buffer):
-        def one(j, acc):
-            other = held[j]
-            parts_of = [
-                jnp.sum(jnp.sum(buffer[me_v * nl + s] * other, axis=0), axis=0, keepdims=True)
-                for s in range(nl)
-            ]
-            value = jnp.sum(jnp.concatenate(parts_of, axis=0), axis=1, keepdims=True)
-            return jnp.where(lane_row == j, value, acc)
-
-        return lax.fori_loop(0, nvec, one, jnp.zeros((nl, depth), jnp.float32), unroll=4)
-
-    def spread(message, inbox, send, recv):
-        inbox[me_g, me_v] = message[...]
-
-        def start(k, carry):
-            remote(message, inbox.at[me_g, me_v], send.at[k], recv.at[me], device_at(k)).start()
-            return carry
-
-        lax.fori_loop(1, total_devices, start, 0)
-
-    def collect(message, inbox, send, recv, slot):
-        def wait(k, carry):
-            g, v = device_at(k)
-            copy = remote(message, inbox.at[g, v], send.at[k], recv.at[g * parts + v], (g, v))
-            copy.wait_recv()
-            copy.wait_send()
-            return carry
-
-        lax.fori_loop(1, total_devices, wait, 0)
-        for v in range(parts):
-            total = inbox[0, v]
-            for g in range(1, groups):
-                total = total + inbox[g, v]
-            mats[slot, v * nl : (v + 1) * nl] = total / (groups * rows * cols * depth)
-
-    trial_copy(0).wait_recv()
-    for q in range(1, pairs):
-        trial_relay(q).wait_recv()
-    gmsg[...] = products(held)
-    spread(gmsg, gin, gsend, grecv)
+                    waves[pair * 2 * nl + me_g] = phi[pl.ds(bx * rows, rows)]
 
     def wave_core(s):
         slot = waves.at[me_v * nl + s]
@@ -407,23 +420,6 @@
     def wave_relay(q, s):
         slot = waves.at[from_pair(q) * nl + s]
         return remote(slot, slot, ysend.at[q, s], yrecv.at[q, s], partner)
-
-    for s in range(nl):
-        @pl.when(jnp.logical_not(own_slot(s)))
-        def _():
-            slot = waves.at[me_v * nl + s]
-            remote(phi.at[0:rows], slot, bsend.at[0], brecv.at[s], partner).wait_recv()
-
-        for q in range(1, pairs):
-            wave_over(q, s).start()
-        wave_core(s).start()
-
-    cmsg[...] = products(waves)
-    spread(cmsg, cin, csend, crecv)
-    for q in range(1, pairs):
-        for s in range(nl):
-            wave_from(q, s).wait_recv()
-            wave_relay(q, s).start()
 
     collect(gmsg, gin, gsend, grecv, 0)
     gram = mats[0]
@@ -441,28 +437,48 @@
     for i in range(nvec):
         coef[i] = jnp.broadcast_to(own_rows[:, i : i + 1], (nl, depth))
 
-    def rotate(buffer, out):
+    def rotate(buffer, out, base, count, fresh):
         def one(row, carry):
-            totals = [None] * nl
-            for i in range(nvec):
-                value = buffer[i, row]
+            totals = [None if fresh else out[s, row] for s in range(nl)]
+            for i in range(count):
+                value = buffer[base + i, row]
                 for s in range(nl):
-                    term = coef[i, s : s + 1] * value
-                    totals[s] = term if i == 0 else totals[s] + term
+                    term = coef[base + i, s : s + 1] * value
+                    totals[s] = term if totals[s] is None else totals[s] + term
             for s in range(nl):
                 out[s, row] = totals[s]
             return carry
 
         lax.fori_loop(0, rows, one, 0)
 
-    rotate(held, rotated)
+    rotate(held, rotated, 0, nvec, True)
+    for s in range(nl):
+        @pl.when(jnp.logical_not(own_slot(s)))
+        def _():
+            slot = waves.at[me_v * nl + s]
+            remote(phi.at[0:rows], slot, bsend.at[0], brecv.at[s], partner).wait_recv()
+
+        for q in range(1, pairs):
+            wave_over(q, s).start()
+        wave_core(s).start()
+        if 2 * (s + 1) == nl:
+            cmsg[: nl // 2] = products(waves, range(nl // 2))
+
+    cmsg[nl // 2 :] = products(waves, range(nl // 2, nl))
+    spread(cmsg, cin, csend, crecv)
+    for q in range(1, pairs):
+        for s in range(nl):
+            wave_from(q, s).wait_recv()
+            wave_relay(q, s).start()
+
     for s in range(nl):
         slot = waves.at[(pair * 2 + 1 - core) * nl + s]
         remote(slot, slot, psend.at[s], precv.at[s], partner).wait_recv()
+    rotate(waves, potentials, pair * 2 * nl, 2 * nl, True)
     for q in range(1, pairs):
         for s in range(nl):
             wave_relay(q, s).wait_recv()
-    rotate(waves, potentials)
+        rotate(waves, potentials, lax.rem(pair - q + pairs, pairs) * 2 * nl, 2 * nl, False)
 
     collect(cmsg, cin, csend, crecv, 2)
     cross = mats[2]
@@ -511,13 +527,14 @@
     return pl.pallas_call(
         functools.partial(kernel, groups, parts),
         out_shape=(
-            jax.ShapeDtypeStruct(trial_block.shape, f32),
-            jax.ShapeDtypeStruct(trial_block.shape, f32),
-            jax.ShapeDtypeStruct((nvec, nvec), f32),
+            pltpu.VMEM(trial_block.shape, f32),
+            pltpu.VMEM(trial_block.shape, f32),
+            pltpu.VMEM((nvec, nvec), f32),
         ),
-        in_specs=[vmem, vmem],
+        in_specs=[pl.BlockSpec(memory_space=pl.ANY)] * 2,
         out_specs=(vmem, vmem, vmem),
         scratch_shapes=[
+            pltpu.VMEM((rows, cols, depth), f32),
             pltpu.VMEM((nl, rows, cols, depth), f32),
             pltpu.VMEM((length, cols + 2 * PAD, depth), f32),
             field, field, field, field, small, small, whole, whole,
@@ -527,7 +544,7 @@
             dma((ITERS,)), dma((ITERS,)), dma((pairs,)), dma((pairs,)), dma((pairs,)), dma((pairs,)),
             dma((blocks,)), dma((nl,)), dma((nl,)), dma((nl,)),
             dma((pairs, nl)), dma((pairs, nl)), dma((pairs, nl)), dma((pairs, nl)),
-            dma((devices,)), dma((devices,)), dma((devices,)), dma((devices,)),
+            dma((devices,)), dma((devices,)), dma((devices,)), dma((devices,)), dma((2,)),
         ],
         compiler_params=pltpu.CompilerParams(collective_id=0, has_side_effects=True),
     )(trial_block, response_weight)

time: 55.5 us -> 49.4 us (0.89)
  the two profiles are of different devices: /device:TPU:1 before, /device:TPU:0 now
where the time goes in v2:
time: 49.4 us; the launch traced here: 49.2 us
  Pallas kernels  46.5 us (94%)
  local copies, waits for them, and re-layouts  2.09 us (4%)
  between operations  0.64 us (1%)
    pallas_call x1, Pallas kernels, paired_body(): pl.pallas_call(functools.partial(kernel, groups, parts), out_shape=(pltpu...  46.5 us
    unnamed x3, local copies, waits for them, and re-layouts  2.09 us

profile of v2, /device:TPU:0, one launch (start us, length us, event | category | flops | bytes accessed | tf_op | source)
XLA Modules:
  0.0 49.2 jit_solution(15605118229534949595)
XLA Ops:
  0.6 46.5 %shard_map.49 = (f32[4,6,32,128]{3,2,1,0:T(8,128)S(1)}, f32[4,6,32,128]{3,2,1,0:T(8,128)S(1)}, f32[16,16]{1,0:T(8,128)S(1)}) custom-call(f32[4,6,32,128]{3,2,1,0:T(8,128)} %trial.1, f32[6,32,128]{2,1,0:T(8,128)} %weight.1), custom_call_target="tpu_custom_call" | custom-call | tf_op jit(solution)/shard_map/pallas_call | solution.py:527
  47.1 0.7 %copy.8 = f32[4,6,32,128]{3,2,1,0:T(8,128)} copy(f32[4,6,32,128]{3,2,1,0:T(8,128)S(1)} %get-tuple-element.3) | data formatting | bytes 786432
  47.9 0.6 %copy.10 = f32[16,16]{1,0:T(8,128)} copy(f32[16,16]{1,0:T(8,128)S(1)} %get-tuple-element.5) | data formatting | bytes 2048
  48.5 0.7 %copy.9 = f32[4,6,32,128]{3,2,1,0:T(8,128)} copy(f32[4,6,32,128]{3,2,1,0:T(8,128)S(1)} %get-tuple-element.4) | data formatting | bytes 786432
